TPU v7x, 256 devices: a whole 4x4x8 slice. The times are simulated.
256 devices in a mesh: row: 16 (over x, y), col: 16 (over z, core).
Axes of the slice: x: 4, y: 4, z: 8, core: 2. Of those that a mesh axis runs over, the one named last changes fastest.
Arguments:
- features: bfloat16 [65536, 256], P(('col', 'row')), may hold values from -6 to 6
- cotangent: bfloat16 [65536, 256], P(('row', 'col')), may hold values from -1.5 to 1.5
- degrees: int32 [65536], P(('row', 'col')), may hold values from 8 to 40
- weight: bfloat16 [256, 256], replicated, may hold values from -0.375 to 0.375
- tile_rows: int32 [16, 16, 256], P('row', 'col'), may hold values from 0 to 31
- tile_cols: int32 [16, 16, 256], P('row', 'col'), may hold values from 0 to 31
- tile_bits: int32 [16, 16, 256, 16, 128], P('row', 'col'), may hold values from 0 to 255, as said below
- tile_count: int32 [16, 16], P('row', 'col'), may hold values from 16 to 256, as said below
Outputs:
- output: bfloat16 [65536, 256], P(('row', 'col'))
- weight_grad: float32 [256, 256], replicated
- input_grad: bfloat16 [65536, 256], P(('col', 'row'))
Inputs may be any that keep to these rules, and one draw needn't show every extreme that they name: `tile_bits`: each word holds 8 entries of 0 or 1 in its low bits; tiles at the same position may repeat and then add. `tile_count`: some device has all 256 slots live and some device 256 // 16.
All inputs are finite; a program needn't handle non-finite values.
Results may differ from a plain program's by a relative error of at most 0.024.
Values may be sent and summed in bfloat16 or wider, within the bound.
No kernel may reach another device: no remote copies, remote signals or barrier semaphores. Data moves between devices by JAX's collectives and lax.ppermute only.
A program may use at most 64 MiB of HBM per device.

v0:
```python
import math

import jax
import jax.numpy as jnp
from jax import lax
from jax.sharding import PartitionSpec as P


def unpack(packed):
    shifts = jnp.arange(8, dtype=jnp.int32)
    flags = jnp.right_shift(packed[:, :, None, :], shifts[None, None, :, None]) & 1
    return flags.reshape(packed.shape[0], packed.shape[1] * 8, packed.shape[2])


def sweep_tiles(packed, row_ids, col_ids, live_count, source, tile_offset, out_tiles, forward):
    tile_size = packed.shape[-1]
    feature_width = source.shape[-1]
    block_size = math.gcd(packed.shape[0], 32)

    def one_block(position, totals):
        offset = position * block_size
        block_bits = lax.dynamic_slice_in_dim(packed, offset, block_size, 0)
        block_rows = lax.dynamic_slice_in_dim(row_ids, offset, block_size, 0)
        block_cols = lax.dynamic_slice_in_dim(col_ids, offset, block_size, 0)
        if forward:
            target = block_rows - tile_offset
        else:
            target = block_cols - tile_offset
        inside = (target >= 0) & (target < out_tiles)
        live_mask = (offset + jnp.arange(block_size, dtype=jnp.int32) < live_count) & inside
        placed = jnp.clip(target, 0, out_tiles - 1)
        pattern = (unpack(block_bits) * live_mask.astype(jnp.int32)[:, None, None]).astype(
            jnp.bfloat16
        )
        if forward:
            product = jnp.einsum(
                "bji,bjf->bif", pattern, source[block_cols], preferred_element_type=jnp.float32
            )
        else:
            product = jnp.einsum(
                "bji,bif->bjf", pattern, source[block_rows], preferred_element_type=jnp.float32
            )
        return totals.at[placed].add(product)

    initial = jnp.zeros((out_tiles, tile_size, feature_width), jnp.float32)
    blocks_used = packed.shape[0] // block_size
    return lax.fori_loop(0, blocks_used, one_block, initial)


def forward_pass(features, degrees, weight, packed, row_ids, col_ids, live_count):
    tile_size = packed.shape[-1]
    width = features.shape[-1]
    gathered = lax.all_gather(features, "row", axis=0, tiled=True)
    source = gathered.reshape(-1, tile_size, width)
    out_tiles = features.shape[0] * lax.axis_size("col") // tile_size
    partial_value = sweep_tiles(packed, row_ids, col_ids, live_count, source, 0, out_tiles, True)
    summed = lax.psum_scatter(
        partial_value.reshape(-1, width).astype(jnp.bfloat16),
        "col",
        scatter_dimension=0,
        tiled=True,
    ).astype(jnp.float32)
    aggregated = (summed / degrees[:, None].astype(jnp.float32)).astype(jnp.bfloat16)
    output = jnp.dot(aggregated, weight, preferred_element_type=jnp.float32).astype(jnp.bfloat16)
    return (aggregated, output)


def backward_pass(cotangent, degrees, weight, packed, row_ids, col_ids, live_count):
    tile_size = packed.shape[-1]
    width = cotangent.shape[-1]
    scaled = (cotangent.astype(jnp.float32) / degrees[:, None].astype(jnp.float32)).astype(
        jnp.bfloat16
    )
    gathered = lax.all_gather(scaled, "col", axis=0, tiled=True)
    source = gathered.reshape(-1, tile_size, width)
    out_tiles = cotangent.shape[0] * lax.axis_size("row") // tile_size
    partial_value = sweep_tiles(packed, row_ids, col_ids, live_count, source, 0, out_tiles, False)
    summed = lax.psum_scatter(
        partial_value.reshape(-1, width).astype(jnp.bfloat16),
        "row",
        scatter_dimension=0,
        tiled=True,
    )
    return jnp.dot(summed, weight.T, preferred_element_type=jnp.float32).astype(jnp.bfloat16)


def per_device(features, cotangent, degrees, weight, tile_rows, tile_cols, tile_bits, tile_count):
    packed = tile_bits[0, 0]
    row_ids = tile_rows[0, 0]
    col_ids = tile_cols[0, 0]
    live_count = tile_count[0, 0]
    aggregated, output = forward_pass(
        features, degrees, weight, packed, row_ids, col_ids, live_count
    )
    input_grad = backward_pass(cotangent, degrees, weight, packed, row_ids, col_ids, live_count)
    local_term = lax.dot_general(
        aggregated, cotangent, (((0,), (0,)), ((), ())), preferred_element_type=jnp.float32
    )
    weight_grad = lax.psum(local_term, ("row", "col"))
    return (output, weight_grad, input_grad)


def solution(mesh):
    placed = (
        P(("col", "row"), None),
        P(("row", "col"), None),
        P(("row", "col")),
        P(),
        P("row", "col", None),
        P("row", "col", None),
        P("row", "col", None, None, None),
        P("row", "col"),
    )
    return jax.shard_map(
        per_device,
        mesh=mesh,
        in_specs=placed,
        out_specs=(P(("row", "col"), None), P(), P(("col", "row"), None)),
        check_vma=False,
    )
```

profile of v0, /device:TPU:1, one launch (start us, length us, event | category | flops | bytes accessed | tf_op | source)
XLA Modules:
  0.0 689.7 jit_solution(7609712674612229882)
XLA Ops:
  10.4 53.0 %all-gather.3.cloned.1.call-done = bf16[4096,256]{1,0:T(8,128)(2,1)} async-done(((bf16[256,256]{1,0:T(8,128)(2,1)}), bf16[4096,256]{1,0:T(8,128)(2,1)}) %all-gather.3.cloned.1.call-update) | async-done | bytes 2097168 | tf_op jit(solution)/shard_map/all_gather | solution.py:53
  65.9 136.1 %while.26 = (s32[]{:T(128)}, f32[32,128,256]{2,1,0:T(8,128)}, s32[256]{0:T(256)S(1)}, s32[256,16,128]{2,1,0:T(8,128)}, s32[]{:T(128)}, /*index=5*/s32[256]{0:T(2...) while((s32[]{:T(128)}, f32[32,128,256]{2,1,0:T(8,128)}, ...), condition=%wide.region_2.3_spmd, body=%wide.region_0.2_spmd.sunk | while | flops 271582656 | bytes 23862704 | solution.py:47
  70.0 2.9 fusion.35
  72.9 9.9 %scatter_fusion = f32[32,128,256]{2,1,0:T(8,128)} fusion(f32[32,128,256]{2,1,0:T(8,128)} %get-tuple-element.398, s32[32]{0:T(128)S(1)} %get-tuple-element.375, f32[32,128,256]{2,1,0:T(8,128)} %fusion.35), kind=kCustom, calls=%fused_computation.2.clone.1 | custom fusion | flops 1048576 | bytes 12583040 | tf_op jit(solution)/shard_map/while/body/eval_jaxpr/scatter-add | solution.py:43
  87.1 2.9 fusion.35
  90.0 9.9 %scatter_fusion = f32[32,128,256]{2,1,0:T(8,128)} fusion(f32[32,128,256]{2,1,0:T(8,128)} %get-tuple-element.398, s32[32]{0:T(128)S(1)} %get-tuple-element.375, f32[32,128,256]{2,1,0:T(8,128)} %fusion.35), kind=kCustom, calls=%fused_computation.2.clone.1 | custom fusion | flops 1048576 | bytes 12583040 | tf_op jit(solution)/shard_map/while/body/eval_jaxpr/scatter-add | solution.py:43
  104.1 2.9 fusion.35
  107.0 9.9 %scatter_fusion = f32[32,128,256]{2,1,0:T(8,128)} fusion(f32[32,128,256]{2,1,0:T(8,128)} %get-tuple-element.398, s32[32]{0:T(128)S(1)} %get-tuple-element.375, f32[32,128,256]{2,1,0:T(8,128)} %fusion.35), kind=kCustom, calls=%fused_computation.2.clone.1 | custom fusion | flops 1048576 | bytes 12583040 | tf_op jit(solution)/shard_map/while/body/eval_jaxpr/scatter-add | solution.py:43
  121.1 2.9 fusion.35
  124.0 10.1 %scatter_fusion = f32[32,128,256]{2,1,0:T(8,128)} fusion(f32[32,128,256]{2,1,0:T(8,128)} %get-tuple-element.398, s32[32]{0:T(128)S(1)} %get-tuple-element.375, f32[32,128,256]{2,1,0:T(8,128)} %fusion.35), kind=kCustom, calls=%fused_computation.2.clone.1 | custom fusion | flops 1048576 | bytes 12583040 | tf_op jit(solution)/shard_map/while/body/eval_jaxpr/scatter-add | solution.py:43
  138.2 2.9 fusion.35
  141.1 10.0 %scatter_fusion = f32[32,128,256]{2,1,0:T(8,128)} fusion(f32[32,128,256]{2,1,0:T(8,128)} %get-tuple-element.398, s32[32]{0:T(128)S(1)} %get-tuple-element.375, f32[32,128,256]{2,1,0:T(8,128)} %fusion.35), kind=kCustom, calls=%fused_computation.2.clone.1 | custom fusion | flops 1048576 | bytes 12583040 | tf_op jit(solution)/shard_map/while/body/eval_jaxpr/scatter-add | solution.py:43
  155.3 2.9 fusion.35
  158.2 9.8 %scatter_fusion = f32[32,128,256]{2,1,0:T(8,128)} fusion(f32[32,128,256]{2,1,0:T(8,128)} %get-tuple-element.398, s32[32]{0:T(128)S(1)} %get-tuple-element.375, f32[32,128,256]{2,1,0:T(8,128)} %fusion.35), kind=kCustom, calls=%fused_computation.2.clone.1 | custom fusion | flops 1048576 | bytes 12583040 | tf_op jit(solution)/shard_map/while/body/eval_jaxpr/scatter-add | solution.py:43
  172.1 2.9 fusion.35
  175.0 10.0 %scatter_fusion = f32[32,128,256]{2,1,0:T(8,128)} fusion(f32[32,128,256]{2,1,0:T(8,128)} %get-tuple-element.398, s32[32]{0:T(128)S(1)} %get-tuple-element.375, f32[32,128,256]{2,1,0:T(8,128)} %fusion.35), kind=kCustom, calls=%fused_computation.2.clone.1 | custom fusion | flops 1048576 | bytes 12583040 | tf_op jit(solution)/shard_map/while/body/eval_jaxpr/scatter-add | solution.py:43
  189.1 2.9 fusion.35
  192.0 9.9 %scatter_fusion = f32[32,128,256]{2,1,0:T(8,128)} fusion(f32[32,128,256]{2,1,0:T(8,128)} %get-tuple-element.398, s32[32]{0:T(128)S(1)} %get-tuple-element.375, f32[32,128,256]{2,1,0:T(8,128)} %fusion.35), kind=kCustom, calls=%fused_computation.2.clone.1 | custom fusion | flops 1048576 | bytes 12583040 | tf_op jit(solution)/shard_map/while/body/eval_jaxpr/scatter-add | solution.py:43
  201.9 3.8 convert_element_type.63
  208.3 134.6 %while.27 = (s32[]{:T(128)}, f32[32,128,256]{2,1,0:T(8,128)}, s32[256]{0:T(256)S(1)}, s32[256,16,128]{2,1,0:T(8,128)}, s32[]{:T(128)}, /*index=5*/s32[256]{0:T(2...) while((s32[]{:T(128)}, f32[32,128,256]{2,1,0:T(8,128)}, ...), condition=%wide.region_7.8_spmd, body=%wide.region_5.7_spmd.sunk | while | flops 271582656 | bytes 23862704 | solution.py:47
  215.2 10.0 %scatter_fusion.1 = f32[32,128,256]{2,1,0:T(8,128)} fusion(f32[32,128,256]{2,1,0:T(8,128)} %get-tuple-element.431, s32[32]{0:T(128)S(1)} %get-tuple-element.384, f32[32,128,256]{2,1,0:T(8,128)} %fusion.38), kind=kCustom, calls=%fused_computation.3.clone.1 | custom fusion | flops 1048576 | bytes 12583040 | tf_op jit(solution)/shard_map/while/body/eval_jaxpr/scatter-add | solution.py:43
  229.4 2.7 fusion.38
  232.1 10.0 %scatter_fusion.1 = f32[32,128,256]{2,1,0:T(8,128)} fusion(f32[32,128,256]{2,1,0:T(8,128)} %get-tuple-element.431, s32[32]{0:T(128)S(1)} %get-tuple-element.384, f32[32,128,256]{2,1,0:T(8,128)} %fusion.38), kind=kCustom, calls=%fused_computation.3.clone.1 | custom fusion | flops 1048576 | bytes 12583040 | tf_op jit(solution)/shard_map/while/body/eval_jaxpr/scatter-add | solution.py:43
  249.0 10.0 %scatter_fusion.1 = f32[32,128,256]{2,1,0:T(8,128)} fusion(f32[32,128,256]{2,1,0:T(8,128)} %get-tuple-element.431, s32[32]{0:T(128)S(1)} %get-tuple-element.384, f32[32,128,256]{2,1,0:T(8,128)} %fusion.38), kind=kCustom, calls=%fused_computation.3.clone.1 | custom fusion | flops 1048576 | bytes 12583040 | tf_op jit(solution)/shard_map/while/body/eval_jaxpr/scatter-add | solution.py:43
  265.9 10.0 %scatter_fusion.1 = f32[32,128,256]{2,1,0:T(8,128)} fusion(f32[32,128,256]{2,1,0:T(8,128)} %get-tuple-element.431, s32[32]{0:T(128)S(1)} %get-tuple-element.384, f32[32,128,256]{2,1,0:T(8,128)} %fusion.38), kind=kCustom, calls=%fused_computation.3.clone.1 | custom fusion | flops 1048576 | bytes 12583040 | tf_op jit(solution)/shard_map/while/body/eval_jaxpr/scatter-add | solution.py:43
  282.8 10.0 %scatter_fusion.1 = f32[32,128,256]{2,1,0:T(8,128)} fusion(f32[32,128,256]{2,1,0:T(8,128)} %get-tuple-element.431, s32[32]{0:T(128)S(1)} %get-tuple-element.384, f32[32,128,256]{2,1,0:T(8,128)} %fusion.38), kind=kCustom, calls=%fused_computation.3.clone.1 | custom fusion | flops 1048576 | bytes 12583040 | tf_op jit(solution)/shard_map/while/body/eval_jaxpr/scatter-add | solution.py:43
  299.6 9.7 %scatter_fusion.1 = f32[32,128,256]{2,1,0:T(8,128)} fusion(f32[32,128,256]{2,1,0:T(8,128)} %get-tuple-element.431, s32[32]{0:T(128)S(1)} %get-tuple-element.384, f32[32,128,256]{2,1,0:T(8,128)} %fusion.38), kind=kCustom, calls=%fused_computation.3.clone.1 | custom fusion | flops 1048576 | bytes 12583040 | tf_op jit(solution)/shard_map/while/body/eval_jaxpr/scatter-add | solution.py:43
  316.2 10.0 %scatter_fusion.1 = f32[32,128,256]{2,1,0:T(8,128)} fusion(f32[32,128,256]{2,1,0:T(8,128)} %get-tuple-element.431, s32[32]{0:T(128)S(1)} %get-tuple-element.384, f32[32,128,256]{2,1,0:T(8,128)} %fusion.38), kind=kCustom, calls=%fused_computation.3.clone.1 | custom fusion | flops 1048576 | bytes 12583040 | tf_op jit(solution)/shard_map/while/body/eval_jaxpr/scatter-add | solution.py:43
  333.0 9.9 %scatter_fusion.1 = f32[32,128,256]{2,1,0:T(8,128)} fusion(f32[32,128,256]{2,1,0:T(8,128)} %get-tuple-element.431, s32[32]{0:T(128)S(1)} %get-tuple-element.384, f32[32,128,256]{2,1,0:T(8,128)} %fusion.38), kind=kCustom, calls=%fused_computation.3.clone.1 | custom fusion | flops 1048576 | bytes 12583040 | tf_op jit(solution)/shard_map/while/body/eval_jaxpr/scatter-add | solution.py:43
  342.9 3.8 convert_element_type.71
  351.4 73.5 %reduce-scatter.5.cloned.1.call-done = bf16[256,256]{1,0:T(8,128)(2,1)} async-done(((bf16[4096,256]{1,0:T(8,128)(2,1)}), bf16[256,256]{1,0:T(8,128)(2,1)}) %reduce-scatter.5.cloned.1.call-update) | async-done | bytes 131088 | tf_op jit(solution)/shard_map/reduce_scatter | solution.py:78
  426.6 254.9 %all-reduce.2.cloned.1.call-done = f32[256,256]{1,0:T(8,128)} async-done(((f32[256,256]{1,0:T(8,128)}), f32[256,256]{1,0:T(8,128)}) %all-reduce.2.cloned.1.call-update) | async-done | bytes 262160 | tf_op jit(solution)/shard_map/psum | solution.py:99
  (147 shorter events, 101.5 us)
Async XLA Ops:
  7.2 342.4 %copy-start = (bf16[256,256]{1,0:T(8,128)(2,1)S(1)}, bf16[256,256]{1,0:T(8,128)(2,1)}, u32[]{:S(2)}) copy-start(bf16[256,256]{1,0:T(8,128)(2,1)} %param.15) | copy-start | bytes 393220
  7.2 56.2 %all-gather.3.cloned.1.call-start = ((), (), s32[]{:S(2)}) async-start(), calls=%async_computation.2 | async-start | bytes 2228224 | tf_op jit(solution)/shard_map/all_gather | solution.py:53
  7.9 197.9 %all-gather.5.cloned.1.call-start = ((), (), s32[]{:S(2)}) async-start(), calls=%async_computation.5 | async-start | bytes 2228224 | tf_op jit(solution)/shard_map/all_gather | solution.py:74
  10.3 336.5 %reduce-scatter.3.cloned.1.call-start = ((), (), s32[]{:S(2)}) async-start(), calls=%async_computation.3 | async-start | bytes 2228224 | tf_op jit(solution)/shard_map/reduce_scatter | solution.py:57
  63.4 2.5 copy-start.2
  63.4 2.5 copy-start.3
  205.8 219.1 %reduce-scatter.5.cloned.1.call-start = ((), (), s32[]{:S(2)}) async-start(), calls=%async_computation.6 | async-start | bytes 2228224 | tf_op jit(solution)/shard_map/reduce_scatter | solution.py:78
  346.7 0.9 copy-start.1
  346.8 334.8 %all-reduce.2.cloned.1.call-start = ((), (), s32[]{:S(2)}) async-start(), calls=%async_computation.4 | async-start | bytes 524288 | tf_op jit(solution)/shard_map/psum | solution.py:99
Sparse Core Ops, SparseCore 0:
  10.4 52.8 all-gather.2
  65.8 40.3 all-gather.4
  205.9 56.5 reduce-scatter.2
  346.9 77.9 reduce-scatter.4
  431.6 249.8 all-reduce.1
where the time goes:
time: 692 us; the launch traced here: 690 us
  waiting for transfers between devices  382 us (55%)
  other arithmetic  182 us (26%)
  local copies, waits for them, and re-layouts  60.9 us (9%)
  matrix products  50.3 us (7%)
  between operations  13.8 us (2%)
    psum x1, waiting for transfers between devices, per_device(): weight_grad = lax.psum(local_term, ('row', 'col'))  255 us
    scatter-add x16, other arithmetic, one_block(): return totals.at[placed].add(product)  159 us
    reduce_scatter x1, waiting for transfers between devices, backward_pass(): lax.psum_scatter(partial_value.reshape(-1, width).astype(jnp.bfloat16), '...  73.5 us
    all_gather x1, waiting for transfers between devices, forward_pass(): gathered = lax.all_gather(features, 'row', axis=0, tiled=True)  53 us
    dot_general x8, matrix products, one_block(): jnp.einsum('bji,bjf->bif', pattern, source[block_cols], preferred_element...  23.2 us
    dot_general x8, matrix products, one_block(): jnp.einsum('bji,bif->bjf', pattern, source[block_rows], preferred_element...  21.6 us
    gather x8, local copies, waits for them, and re-layouts, one_block(): source[block_rows]  18.2 us
    gather x8, local copies, waits for them, and re-layouts, one_block(): source[block_cols]  18.2 us
  transfers between devices with their start and end apart: 5, of which 3 were waited for; matrix products, arithmetic and copies ran while one was open for 42% of the time, Pallas kernels for 0%

commit v1 on v0

v1 whole, which is shorter than its diff:
```python
import functools

import jax
import jax.numpy as jnp
from jax import lax
from jax.experimental import pallas as pl
from jax.experimental.pallas import tpu as pltpu
from jax.sharding import PartitionSpec as P

BLOCK = 64
VMEM = 56 << 20


def unpack(words):
    depth, tile = words.shape
    bit = jnp.left_shift(1, lax.broadcasted_iota(jnp.int32, (1, 8, tile), 1))
    wide = jnp.broadcast_to(words[:, None, :], (depth, 8, tile))
    return jnp.where((wide & bit) != 0, 1.0, 0.0).reshape(depth * 8, tile)


def add_tiles(count_ref, to_ref, from_ref, bits_ref, source_ref, total, contract):
    step = pl.program_id(0)
    block = bits_ref.shape[0]

    @pl.when(step == 0)
    def _():
        total[...] = jnp.zeros_like(total)

    @pl.when(step * block < count_ref[0])
    def _():
        for k in range(block):
            slot = step * block + k
            product = lax.dot_general(
                unpack(bits_ref[k]).astype(jnp.bfloat16),
                source_ref[from_ref[slot]],
                (((contract,), (0,)), ((), ())),
                preferred_element_type=jnp.float32,
            )
            total[to_ref[slot]] += product


def forward_body(count_ref, to_ref, from_ref, bits_ref, source_ref, own_ref, other_ref, total):
    add_tiles(count_ref, to_ref, from_ref, bits_ref, source_ref, total, 0)

    @pl.when(pl.program_id(0) == pl.num_programs(0) - 1)
    def _():
        blocks = own_ref.shape[0]
        own_ref[...] = total[:blocks].astype(own_ref.dtype)
        other_ref[...] = total[blocks : 2 * blocks].astype(other_ref.dtype)


def forward_sweep(count, to_ids, from_ids, bits, source):
    slots, depth, tile = bits.shape
    blocks, _, width = source.shape
    out = jax.ShapeDtypeStruct((blocks // 2, tile, width), jnp.bfloat16)
    out_spec = pl.BlockSpec(out.shape, lambda i, *_: (0, 0, 0))
    return pl.pallas_call(
        forward_body,
        out_shape=(out, out),
        grid_spec=pltpu.PrefetchScalarGridSpec(
            num_scalar_prefetch=3,
            grid=(slots // BLOCK,),
            in_specs=[
                pl.BlockSpec((BLOCK, depth, tile), lambda i, *_: (i, 0, 0)),
                pl.BlockSpec(source.shape, lambda i, *_: (0, 0, 0)),
            ],
            out_specs=(out_spec, out_spec),
            scratch_shapes=[pltpu.VMEM((blocks + 1, tile, width), jnp.float32)],
        ),
        compiler_params=pltpu.CompilerParams(vmem_limit_bytes=VMEM),
        cost_estimate=pl.CostEstimate(
            flops=slots * tile * tile * width * 2,
            bytes_accessed=bits.size * 4 + source.size * 4,
            transcendentals=0,
        ),
        name="forward_sweep",
    )(count, to_ids, from_ids, bits, source)


def backward_body(count_ref, to_ref, from_ref, bits_ref, source_ref, out_ref, total):
    add_tiles(count_ref, to_ref, from_ref, bits_ref, source_ref, total, 1)

    @pl.when(pl.program_id(0) == pl.num_programs(0) - 1)
    def _():
        out_ref[...] = total[: out_ref.shape[0]].astype(out_ref.dtype)


def backward_sweep(count, to_ids, from_ids, bits, source):
    slots, depth, tile = bits.shape
    blocks, _, width = source.shape
    out = jax.ShapeDtypeStruct((blocks, tile, width), jnp.bfloat16)
    return pl.pallas_call(
        backward_body,
        out_shape=out,
        grid_spec=pltpu.PrefetchScalarGridSpec(
            num_scalar_prefetch=3,
            grid=(slots // BLOCK,),
            in_specs=[
                pl.BlockSpec((BLOCK, depth, tile), lambda i, *_: (i, 0, 0)),
                pl.BlockSpec(source.shape, lambda i, *_: (0, 0, 0)),
            ],
            out_specs=pl.BlockSpec(out.shape, lambda i, *_: (0, 0, 0)),
            scratch_shapes=[pltpu.VMEM((blocks + 1, tile, width), jnp.float32)],
        ),
        compiler_params=pltpu.CompilerParams(vmem_limit_bytes=VMEM),
        cost_estimate=pl.CostEstimate(
            flops=slots * tile * tile * width * 2,
            bytes_accessed=bits.size * 4 + source.size * 4,
            transcendentals=0,
        ),
        name="backward_sweep",
    )(count, to_ids, from_ids, bits, source)


def pack_body(partial_ref, features_ref, out_ref):
    owners, rows, width = out_ref.shape
    nodes = partial_ref.shape[1]
    term = jnp.zeros((width, width), jnp.float32)
    for owner in range(owners):
        part = partial_ref[owner]
        out_ref[owner, :nodes] = part
        term += lax.dot_general(
            features_ref[owner], part, (((0,), (0,)), ((), ())), preferred_element_type=jnp.float32
        )
    for owner in range(owners):
        share = term[owner * (rows - nodes) : (owner + 1) * (rows - nodes)]
        out_ref[owner, nodes:] = share.astype(out_ref.dtype)


def pack(partial, features):
    owners, nodes, width = features.shape
    out = jax.ShapeDtypeStruct((owners, nodes + width // owners, width), jnp.bfloat16)
    whole = pl.BlockSpec(memory_space=pltpu.VMEM)
    return pl.pallas_call(
        pack_body,
        out_shape=out,
        in_specs=[whole, whole],
        out_specs=whole,
        cost_estimate=pl.CostEstimate(
            flops=features.size * width * 2, bytes_accessed=features.size * 6, transcendentals=0
        ),
        name="pack",
    )(partial, features)


def spread(block, axis):
    copies = lax.axis_size(axis)
    return lax.all_to_all(jnp.broadcast_to(block[None], (copies, *block.shape)), axis, 0, 0)


def swap_cores(block):
    return lax.ppermute(block, "col", [(i, i ^ 1) for i in range(lax.axis_size("col"))])


def swap_chips(block):
    return lax.ppermute(block, "col", [(i, i ^ 2) for i in range(lax.axis_size("col"))])


def from_below(block, distance):
    n_col = lax.axis_size("col")
    return lax.ppermute(block, "col", [(i, (i + 2 * distance) % n_col) for i in range(n_col)])


def per_device(features, cotangent, degrees, weight, tile_rows, tile_cols, tile_bits, tile_count):
    row_ids, col_ids, count = tile_rows[0, 0], tile_cols[0, 0], tile_count[0]
    tile = tile_bits.shape[-1]
    nodes, width = features.shape
    n_row, n_col = lax.axis_size("row"), lax.axis_size("col")
    n_z = n_col // 2
    place = lax.axis_index("col")
    core, z = place % 2, place // 2
    core_id = core.astype(jnp.int32)[None]
    degree = degrees[:, None].astype(jnp.float32)

    bits = tile_bits[0, 0]
    blocks = n_row * nodes // tile

    copies = jnp.broadcast_to(features[None], (n_row, nodes, width))
    source = lax.all_to_all(copies, "row", 0, 0)
    scaled = (cotangent.astype(jnp.float32) / degree).astype(jnp.bfloat16)
    own = jnp.stack([scaled] + [from_below(scaled, d) for d in range(1, n_z)])
    gradient = jnp.concatenate([own, swap_cores(own)])

    live = jnp.arange(row_ids.shape[0], dtype=jnp.int32) < count
    owner, half = row_ids // 2, row_ids % 2
    side = (owner % 2 != core) * n_z
    row_sources = (side + jnp.remainder(z - owner // 2, n_z)) * 2 + half
    apart = (owner // 2 + z) % 2 * (n_z // 2)
    away = jnp.remainder(owner // 4 - z // 2, n_z // 2)
    row_targets = (side + apart + away) * 2 + half
    row_targets = jnp.where(live, row_targets, blocks)
    col_targets = jnp.where(live, col_ids, blocks)

    partial = backward_sweep(
        count, col_targets, row_sources, bits, gradient.reshape(-1, tile, width)
    )
    partial = pack(partial.reshape(n_row, nodes, width), source)
    shares = lax.all_to_all(partial, "row", 0, 0)

    kept, sent = forward_sweep(count, row_targets, col_ids, bits, source.reshape(-1, tile, width))
    chip = kept.astype(jnp.float32) + swap_cores(sent).astype(jnp.float32)
    chip = chip.reshape(2, n_z // 2, nodes, width)
    got = swap_chips(chip[1].astype(jnp.bfloat16))
    pair = (chip[0] + got.astype(jnp.float32)).astype(jnp.bfloat16)
    pieces = [pair[0]] + [from_below(pair[k], 2 * k) for k in range(1, n_z // 2)]
    summed = sum(p.astype(jnp.float32) for p in pieces)

    shares = shares.astype(jnp.float32).sum(0)
    term = spread(shares[nodes:], "col").sum(0)
    weight_grad = spread(term, "row").reshape(width, width)
    propagated = shares[:nodes].astype(jnp.bfloat16)
    input_grad = jnp.dot(propagated, weight.T, preferred_element_type=jnp.float32).astype(
        jnp.bfloat16
    )
    aggregated = (summed / degree).astype(jnp.bfloat16)
    output = jnp.dot(aggregated, weight, preferred_element_type=jnp.float32).astype(jnp.bfloat16)
    return output, weight_grad, input_grad


def solution(mesh):
    placed = (
        P(("col", "row"), None),
        P(("row", "col"), None),
        P(("row", "col")),
        P(),
        P("row", "col", None),
        P("row", "col", None),
        P("row", "col", None, None, None),
        P("row", "col"),
    )
    return jax.shard_map(
        per_device,
        mesh=mesh,
        in_specs=placed,
        out_specs=(P(("row", "col"), None), P(), P(("col", "row"), None)),
        check_vma=False,
    )
```

time: 692 us -> 134 us (0.19)
  waiting for transfers between devices: 382 us -> 28.5 us
  other arithmetic: 182 us -> 6.55 us
  starting transfers between devices: 0.2 us -> 56.7 us
  matrix products: 50.3 us -> 1.77 us
  local copies, waits for them, and re-layouts: 60.9 us -> 14.5 us
  Pallas kernels: 0 us -> 24.1 us
  between operations: 13.8 us -> 1.43 us
    psum x1 -> x0, waiting for transfers between devices: 255 us -> none  [per_device(): weight_grad = lax.psum(local_term, ('row', 'col'))]
    scatter-add x16 -> x0, other arithmetic: 159 us -> none  [one_block(): return totals.at[placed].add(product)]
    reduce_scatter x2 -> x0, waiting for transfers between devices: 73.5 us -> none  [the longest x1 73.5 us: backward_pass(): lax.psum_scatter(partial_value.reshape(-1, width).astype(jnp.bfloat16), '...]
    all_gather x2 -> x0, waiting for transfers between devices: 53 us -> none  [the longest x1 53 us: forward_pass(): gathered = lax.all_gather(features, 'row', axis=0, tiled=True)]
    dot_general x19 -> x2, matrix products: 50.3 us -> 1.77 us  [the longest x1 0.89 us: per_device(): jnp.dot(aggregated, weight, preferred_element_type=jnp.float32)]
    gather x16 -> x0, local copies, waits for them, and re-layouts: 36.4 us -> none  [the longest x8 18.2 us: one_block(): source[block_rows]]
    ppermute x0 -> x13, starting transfers between devices: none -> 30.6 us  [the longest x10 26.2 us: from_below(): lax.ppermute(block, 'col', [(i, (i + 2 * distance) % n_col) for i in rang...]
    all_to_all x0 -> x4, starting transfers between devices: none -> 26.1 us  [the longest x2 12.6 us: spread(): lax.all_to_all(jnp.broadcast_to(block[None], (copies, *block.shape)), axi...]
  transfers between devices with their start and end apart: 5 -> 17, of which waited for: 3 -> 8; matrix products, arithmetic and copies ran while one was open for 42% -> 13% of each run, Pallas kernels for 0% -> 15%
where the time goes in v1:
time: 134 us
  starting transfers between devices  56.7 us (42%)
  waiting for transfers between devices  28.5 us (21%)
  Pallas kernels  24.1 us (18%)
  local copies, waits for them, and re-layouts  14.5 us (11%)
  other arithmetic  6.55 us (5%)
  matrix products  1.77 us (1%)
  between operations  1.43 us (1%)
    ppermute x10, starting transfers between devices, from_below(): lax.ppermute(block, 'col', [(i, (i + 2 * distance) % n_col) for i in rang...  26.2 us
    all_to_all x1, waiting for transfers between devices, per_device(): shares = lax.all_to_all(partial, 'row', 0, 0)  13.5 us
    all_to_all x2, starting transfers between devices, spread(): lax.all_to_all(jnp.broadcast_to(block[None], (copies, *block.shape)), axi...  12.6 us
    pallas_call x1, Pallas kernels, forward_sweep(): pl.pallas_call(forward_body, out_shape=(out, out), grid_spec=pltpu.Prefet...  10 us
    pallas_call x1, Pallas kernels, backward_sweep(): pl.pallas_call(backward_body, out_shape=out, grid_spec=pltpu.PrefetchScal...  9.72 us
    unnamed x20, local copies, waits for them, and re-layouts  7.81 us
    all_to_all x2, waiting for transfers between devices, spread(): lax.all_to_all(jnp.broadcast_to(block[None], (copies, *block.shape)), axi...  7.19 us
    all_to_all x1, starting transfers between devices, per_device(): shares = lax.all_to_all(partial, 'row', 0, 0)  6.79 us
  transfers between devices with their start and end apart: 17, of which 8 were waited for; matrix products, arithmetic and copies ran while one was open for 13% of the time, Pallas kernels for 15%

profile of v1, /device:TPU:1, one launch (start us, length us, event | category | flops | bytes accessed | tf_op | source)
XLA Modules:
  0.0 133.5 jit_solution(747488867802112887)
XLA Ops:
  1.4 1.7 %bitcast_dynamic-update-slice_fusion.15 = (bf16[8,256,256]{2,1,0:T(8,128)(2,1)}, bf16[256,256]{1,0:T(8,128)(2,1)S(1)}) fusion(f32[256]{0:T(256)S(1)} %convert_element_type.65, bf16[256,256]{1,0:T(8,128)(2,1)} %param.9), kind=kLoop, calls=%fused_computation.33 | loop fusion | flops 196607 | bytes 394240
  3.0 2.5 %collective-permute-start.5 = (bf16[256,256]{1,0:T(8,128)(2,1)S(1)}, bf16[256,256]{1,0:T(8,128)(2,1)S(1)}, u32[]{:S(2)}, u32[]{:S(2)}) collective-permute-start(bf16[256,256]{1,0:T(8,128)(2,1)S(1)} %get-tuple-element.8), channel_id=1, source_target_pairs={{0,2},{1,3},{2,4},{3,5},{4,6},{5,7},{6,8},{7,9},{8,10},{9,11},{10,... | collective-permute-start | bytes 393224 | tf_op jit(solution)/shard_map/ppermute | solution.py:161
  5.5 3.0 %collective-permute-start.6 = (bf16[256,256]{1,0:T(8,128)(2,1)S(1)}, bf16[256,256]{1,0:T(8,128)(2,1)S(1)}, u32[]{:S(2)}, u32[]{:S(2)}) collective-permute-start(bf16[256,256]{1,0:T(8,128)(2,1)S(1)} %get-tuple-element.8), channel_id=1, source_target_pairs={{0,4},{1,5},{2,6},{3,7},{4,8},{5,9},{6,10},{7,11},{8,12},{9,13},{1... | collective-permute-start | bytes 393224 | tf_op jit(solution)/shard_map/ppermute | solution.py:161
  8.5 3.8 %collective-permute-start.7 = (bf16[256,256]{1,0:T(8,128)(2,1)S(1)}, bf16[256,256]{1,0:T(8,128)(2,1)S(1)}, u32[]{:S(2)}, u32[]{:S(2)}) collective-permute-start(bf16[256,256]{1,0:T(8,128)(2,1)S(1)} %get-tuple-element.8), channel_id=1, source_target_pairs={{0,6},{1,7},{2,8},{3,9},{4,10},{5,11},{6,12},{7,13},{8,14},{9,15},... | collective-permute-start | bytes 393224 | tf_op jit(solution)/shard_map/ppermute | solution.py:161
  12.7 4.5 %collective-permute-start.9 = (bf16[256,256]{1,0:T(8,128)(2,1)S(1)}, bf16[256,256]{1,0:T(8,128)(2,1)S(1)}, u32[]{:S(2)}, u32[]{:S(2)}) collective-permute-start(bf16[256,256]{1,0:T(8,128)(2,1)S(1)} %get-tuple-element.8), channel_id=1, source_target_pairs={{0,10},{1,11},{2,12},{3,13},{4,14},{5,15},{6,0},{7,1},{8,2},{9,3},... | collective-permute-start | bytes 393224 | tf_op jit(solution)/shard_map/ppermute | solution.py:161
  17.2 2.5 %broadcast_in_dim.12 = bf16[16,256,256]{2,1,0:T(8,128)(2,1)} broadcast(bf16[256,256]{1,0:T(8,128)(2,1)} %param.8), dimensions={1,2} | broadcast | bytes 2228224 | tf_op jit(solution)/shard_map/broadcast_in_dim | solution.py:178
  19.7 6.8 %all-to-all-start = ((bf16[16,256,256]{2,1,0:T(8,128)(2,1)}), bf16[16,256,256]{2,1,0:T(8,128)(2,1)S(1)}, u32[]{:S(2)}, u32[]{:S(2)}) async-start(bf16[16,256,256]{2,1,0:T(8,128)(2,1)} %broadcast_in_dim.12), calls=%async_computation | async-start | bytes 4194304 | tf_op jit(solution)/shard_map/all_to_all | solution.py:179
  27.1 2.4 %collective-permute-start.10 = (bf16[256,256]{1,0:T(8,128)(2,1)S(1)}, bf16[256,256]{1,0:T(8,128)(2,1)S(1)}, u32[]{:S(2)}, u32[]{:S(2)}) collective-permute-start(bf16[256,256]{1,0:T(8,128)(2,1)S(1)} %get-tuple-element.8), channel_id=1, source_target_pairs={{0,12},{1,13},{2,14},{3,15},{4,0},{5,1},{6,2},{7,3},{8,4},{9,5},{1... | collective-permute-start | bytes 393224 | tf_op jit(solution)/shard_map/ppermute | solution.py:161
  33.9 2.2 %collective-permute-done.10 = bf16[256,256]{1,0:T(8,128)(2,1)S(1)} collective-permute-done((bf16[256,256]{1,0:T(8,128)(2,1)S(1)}, bf16[256,256]{1,0:T(8,128)(2,1)S(1)}, u32[]{:S(2)}, u32[]{:S(2)}) %collective-permute-start.10) | collective-permute-done | bytes 131104 | tf_op jit(solution)/shard_map/ppermute | solution.py:161
  36.8 1.0 collective-permute-done.11
  38.5 2.3 %collective-permute-start.12 = (bf16[8,256,256]{2,1,0:T(8,128)(2,1)}, bf16[8,256,256]{2,1,0:T(8,128)(2,1)S(1)}, u32[]{:S(2)}, u32[]{:S(2)}) collective-permute-start(bf16[8,256,256]{2,1,0:T(8,128)(2,1)} %get-tuple-element.12), channel_id=1, source_target_pairs={{0,1},{1,0},{2,3},{3,2},{4,5},{5,4},{6,7},{7,6},{8,9},{9,8},{10,11... | collective-permute-start | bytes 3145736 | tf_op jit(solution)/shard_map/ppermute | solution.py:152
  43.3 1.0 constant_dynamic-update-slice_fusion
  44.4 9.7 %backward_sweep.1 = bf16[32,128,256]{2,1,0:T(8,128)(2,1)} custom-call(s32[1]{0:T(128)} %bitcast.54.count_ref, s32[256]{0:T(256)} %fusion.13.to_ref, s32[256]{0:T(256)} %get-tuple-element.26.from_ref, s32[256,16,128]{2,1,0:T(8,128)} %bitcast.64, bf16[32,128,256]{2,1,0:T(8,128)(2,1)} %bitcast.20.source_ref), custom_call_target="tpu_custom_call" | custom-call | flops 2147483648 | bytes 6291456 | tf_op jit(solution)/shard_map/backward_sweep/pallas_call | solution.py:92
  54.1 1.3 %copy-done.1 = bf16[16,256,256]{2,1,0:T(8,128)(2,1)} copy-done((bf16[16,256,256]{2,1,0:T(8,128)(2,1)}, bf16[16,256,256]{2,1,0:T(8,128)(2,1)S(1)}, u32[]{:S(2)}) %copy-start.1) | copy-done | bytes 2097176
  55.5 4.4 %pack.1 = bf16[16,272,256]{2,1,0:T(8,128)(2,1)} custom-call(bf16[16,256,256]{2,1,0:T(8,128)(2,1)} %bitcast.59, bf16[16,256,256]{2,1,0:T(8,128)(2,1)} %copy-done.1), custom_call_target="tpu_custom_call" | custom-call | flops 536870912 | bytes 6291456 | tf_op jit(solution)/shard_map/pack/pallas_call | solution.py:134
  59.8 6.8 %all-to-all-start.1 = ((bf16[16,272,256]{2,1,0:T(8,128)(2,1)}), bf16[16,272,256]{2,1,0:T(8,128)(2,1)S(1)}, u32[]{:S(2)}, u32[]{:S(2)}) async-start(bf16[16,272,256]{2,1,0:T(8,128)(2,1)} %pack.1), calls=%async_computation.1 | async-start | bytes 4456448 | tf_op jit(solution)/shard_map/all_to_all | solution.py:198
  66.6 10.0 %forward_sweep.1 = (bf16[16,128,256]{2,1,0:T(8,128)(2,1)}, bf16[16,128,256]{2,1,0:T(8,128)(2,1)}) custom-call(s32[1]{0:T(128)} %bitcast.53.count_ref, s32[256]{0:T(256)} %get-tuple-element.27.to_ref, s32[256]{0:T(256)} %bitcast.62, s32[256,16,128]{2,1,0:T(8,128)} %bitcast.65, bf16[32,128,256]{2,1,0:T(8,128)(2,1)} %bitcast.57), custom_call_target="tpu_custom_call" | custom-call | flops 2147483648 | bytes 6291456 | tf_op jit(solution)/shard_map/forward_sweep/pallas_call | solution.py:57
  77.0 2.5 %collective-permute-done = bf16[16,128,256]{2,1,0:T(8,128)(2,1)S(1)} collective-permute-done((bf16[16,128,256]{2,1,0:T(8,128)(2,1)}, bf16[16,128,256]{2,1,0:T(8,128)(2,1)S(1)}, u32[]{:S(2)}, u32[]{:S(2)}) %collective-permute-start) | collective-permute-done | bytes 1048608 | tf_op jit(solution)/shard_map/ppermute | solution.py:152
  79.5 1.5 %convert_add_fusion = f32[16,128,256]{2,1,0:T(8,128)S(1)} fusion(bf16[16,128,256]{2,1,0:T(8,128)(2,1)S(1)} %collective-permute-done, bf16[16,128,256]{2,1,0:T(8,128)(2,1)} %get-tuple-element.5), kind=kLoop, calls=%fused_computation.1 | loop fusion | flops 1572864 | bytes 4194304 | tf_op jit(solution)/shard_map/add | solution.py:201
  81.9 1.7 %collective-permute-start.1 = (bf16[4,256,256]{2,1,0:T(8,128)(2,1)}, bf16[4,256,256]{2,1,0:T(8,128)(2,1)}, u32[]{:S(2)}, u32[]{:S(2)}) collective-permute-start(bf16[4,256,256]{2,1,0:T(8,128)(2,1)} %bitcast.7), channel_id=1, source_target_pairs={{0,2},{1,3},{2,0},{3,1},{4,6},{5,7},{6,4},{7,5},{8,10},{9,11},{10,... | collective-permute-start | bytes 1572872 | tf_op jit(solution)/shard_map/ppermute | solution.py:156
  83.7 13.5 %all-to-all-done.1 = bf16[16,272,256]{2,1,0:T(8,128)(2,1)S(1)} async-done(((bf16[16,272,256]{2,1,0:T(8,128)(2,1)}), bf16[16,272,256]{2,1,0:T(8,128)(2,1)S(1)}, u32[]{:S(2)}, u32[]{:S(2)}) %all-to-all-start.1) | async-done | bytes 2228256 | tf_op jit(solution)/shard_map/all_to_all | solution.py:198
  98.9 6.0 %all-to-all-start.2 = ((f32[16,16,256]{2,1,0:T(8,128)}), f32[16,16,256]{2,1,0:T(8,128)S(1)}, u32[]{:S(2)}, u32[]{:S(2)}) async-start(f32[16,16,256]{2,1,0:T(8,128)} %broadcast_in_dim.13), calls=%async_computation.2 | async-start | bytes 524288 | tf_op jit(solution)/shard_map/all_to_all | solution.py:148
  104.9 1.2 fusion
  106.1 2.4 %collective-permute-start.2 = (bf16[256,256]{1,0:T(8,128)(2,1)S(1)}, bf16[256,256]{1,0:T(8,128)(2,1)S(1)}, u32[]{:S(2)}, u32[]{:S(2)}) collective-permute-start(bf16[256,256]{1,0:T(8,128)(2,1)S(1)} %get-tuple-element.9), channel_id=1, source_target_pairs={{0,4},{1,5},{2,6},{3,7},{4,8},{5,9},{6,10},{7,11},{8,12},{9,13},{1... | collective-permute-start | bytes 393224 | tf_op jit(solution)/shard_map/ppermute | solution.py:161
  108.5 3.3 %collective-permute-start.3 = (bf16[256,256]{1,0:T(8,128)(2,1)S(1)}, bf16[256,256]{1,0:T(8,128)(2,1)S(1)}, u32[]{:S(2)}, u32[]{:S(2)}) collective-permute-start(bf16[256,256]{1,0:T(8,128)(2,1)S(1)} %get-tuple-element.11), channel_id=1, source_target_pairs={{0,8},{1,9},{2,10},{3,11},{4,12},{5,13},{6,14},{7,15},{8,0},{9,1},... | collective-permute-start | bytes 393224 | tf_op jit(solution)/shard_map/ppermute | solution.py:161
  111.8 3.3 %collective-permute-start.4 = (bf16[256,256]{1,0:T(8,128)(2,1)S(1)}, bf16[256,256]{1,0:T(8,128)(2,1)S(1)}, u32[]{:S(2)}, u32[]{:S(2)}) collective-permute-start(bf16[256,256]{1,0:T(8,128)(2,1)S(1)} %get-tuple-element.10), channel_id=1, source_target_pairs={{0,12},{1,13},{2,14},{3,15},{4,0},{5,1},{6,2},{7,3},{8,4},{9,5},{1... | collective-permute-start | bytes 393224 | tf_op jit(solution)/shard_map/ppermute | solution.py:161
  115.1 1.9 %all-to-all-done.2 = f32[16,16,256]{2,1,0:T(8,128)S(1)} async-done(((f32[16,16,256]{2,1,0:T(8,128)}), f32[16,16,256]{2,1,0:T(8,128)S(1)}, u32[]{:S(2)}, u32[]{:S(2)}) %all-to-all-start.2) | async-done | bytes 262176 | tf_op jit(solution)/shard_map/all_to_all | solution.py:148
  117.7 6.6 %all-to-all-start.3 = ((f32[16,16,256]{2,1,0:T(8,128)}), f32[16,16,256]{2,1,0:T(8,128)S(1)}, u32[]{:S(2)}, u32[]{:S(2)}) async-start(f32[16,16,256]{2,1,0:T(8,128)} %broadcast_in_dim.14), calls=%async_computation.3 | async-start | bytes 524288 | tf_op jit(solution)/shard_map/all_to_all | solution.py:148
  124.3 1.4 %collective-permute-done.3 = bf16[256,256]{1,0:T(8,128)(2,1)S(1)} collective-permute-done((bf16[256,256]{1,0:T(8,128)(2,1)S(1)}, bf16[256,256]{1,0:T(8,128)(2,1)S(1)}, u32[]{:S(2)}, u32[]{:S(2)}) %collective-permute-start.3) | collective-permute-done | bytes 131104 | tf_op jit(solution)/shard_map/ppermute | solution.py:161
  125.7 0.9 convolution_convert_fusion.1
  126.6 0.9 convolution_convert_fusion
  127.5 5.3 %all-to-all-done.3 = f32[16,16,256]{2,1,0:T(8,128)S(1)} async-done(((f32[16,16,256]{2,1,0:T(8,128)}), f32[16,16,256]{2,1,0:T(8,128)S(1)}, u32[]{:S(2)}, u32[]{:S(2)}) %all-to-all-start.3) | async-done | bytes 262176 | tf_op jit(solution)/shard_map/all_to_all | solution.py:148
  (44 shorter events, 14.1 us)
Async XLA Ops:
  0.6 125.1 %copy-start = (bf16[256,256]{1,0:T(8,128)(2,1)S(1)}, bf16[256,256]{1,0:T(8,128)(2,1)}, u32[]{:S(2)}) copy-start(bf16[256,256]{1,0:T(8,128)(2,1)} %param.11) | copy-start | bytes 393220
  3.0 24.1 %collective-permute-start.5 = (bf16[256,256]{1,0:T(8,128)(2,1)S(1)}, bf16[256,256]{1,0:T(8,128)(2,1)S(1)}, u32[]{:S(2)}, u32[]{:S(2)}) collective-permute-start(bf16[256,256]{1,0:T(8,128)(2,1)S(1)} %get-tuple-element.8), channel_id=1, source_target_pairs={{0,2},{1,3},{2,4},{3,5},{4,6},{5,7},{6,8},{7,9},{8,10},{9,11},{10,... | collective-permute-start | bytes 393224 | tf_op jit(solution)/shard_map/ppermute | solution.py:161
  5.5 24.7 %collective-permute-start.6 = (bf16[256,256]{1,0:T(8,128)(2,1)S(1)}, bf16[256,256]{1,0:T(8,128)(2,1)S(1)}, u32[]{:S(2)}, u32[]{:S(2)}) collective-permute-start(bf16[256,256]{1,0:T(8,128)(2,1)S(1)} %get-tuple-element.8), channel_id=1, source_target_pairs={{0,4},{1,5},{2,6},{3,7},{4,8},{5,9},{6,10},{7,11},{8,12},{9,13},{1... | collective-permute-start | bytes 393224 | tf_op jit(solution)/shard_map/ppermute | solution.py:161
  8.5 23.2 %collective-permute-start.7 = (bf16[256,256]{1,0:T(8,128)(2,1)S(1)}, bf16[256,256]{1,0:T(8,128)(2,1)S(1)}, u32[]{:S(2)}, u32[]{:S(2)}) collective-permute-start(bf16[256,256]{1,0:T(8,128)(2,1)S(1)} %get-tuple-element.8), channel_id=1, source_target_pairs={{0,6},{1,7},{2,8},{3,9},{4,10},{5,11},{6,12},{7,13},{8,14},{9,15},... | collective-permute-start | bytes 393224 | tf_op jit(solution)/shard_map/ppermute | solution.py:161
  12.3 20.2 %collective-permute-start.8 = (bf16[256,256]{1,0:T(8,128)(2,1)S(1)}, bf16[256,256]{1,0:T(8,128)(2,1)S(1)}, u32[]{:S(2)}, u32[]{:S(2)}) collective-permute-start(bf16[256,256]{1,0:T(8,128)(2,1)S(1)} %get-tuple-element.8), channel_id=1, source_target_pairs={{0,8},{1,9},{2,10},{3,11},{4,12},{5,13},{6,14},{7,15},{8,0},{9,1},... | collective-permute-start | bytes 393224 | tf_op jit(solution)/shard_map/ppermute | solution.py:161
  12.7 20.4 %collective-permute-start.9 = (bf16[256,256]{1,0:T(8,128)(2,1)S(1)}, bf16[256,256]{1,0:T(8,128)(2,1)S(1)}, u32[]{:S(2)}, u32[]{:S(2)}) collective-permute-start(bf16[256,256]{1,0:T(8,128)(2,1)S(1)} %get-tuple-element.8), channel_id=1, source_target_pairs={{0,10},{1,11},{2,12},{3,13},{4,14},{5,15},{6,0},{7,1},{8,2},{9,3},... | collective-permute-start | bytes 393224 | tf_op jit(solution)/shard_map/ppermute | solution.py:161
  19.7 34.5 %all-to-all-start = ((bf16[16,256,256]{2,1,0:T(8,128)(2,1)}), bf16[16,256,256]{2,1,0:T(8,128)(2,1)S(1)}, u32[]{:S(2)}, u32[]{:S(2)}) async-start(bf16[16,256,256]{2,1,0:T(8,128)(2,1)} %broadcast_in_dim.12), calls=%async_computation | async-start | bytes 4194304 | tf_op jit(solution)/shard_map/all_to_all | solution.py:179
  26.4 15.1 %copy-start.5 = (s32[1,1,256]{2,1,0:T(1,128)S(1)}, s32[1,1,256]{2,1,0:T(1,128)}, u32[]{:S(2)}) copy-start(s32[1,1,256]{2,1,0:T(1,128)} %param.13) | copy-start | bytes 3076
  26.4 15.7 %copy-start.4 = (s32[1,1,256]{2,1,0:T(1,128)S(1)}, s32[1,1,256]{2,1,0:T(1,128)}, u32[]{:S(2)}) copy-start(s32[1,1,256]{2,1,0:T(1,128)} %param.12) | copy-start | bytes 3076
  27.1 8.9 %collective-permute-start.10 = (bf16[256,256]{1,0:T(8,128)(2,1)S(1)}, bf16[256,256]{1,0:T(8,128)(2,1)S(1)}, u32[]{:S(2)}, u32[]{:S(2)}) collective-permute-start(bf16[256,256]{1,0:T(8,128)(2,1)S(1)} %get-tuple-element.8), channel_id=1, source_target_pairs={{0,12},{1,13},{2,14},{3,15},{4,0},{5,1},{6,2},{7,3},{8,4},{9,5},{1... | collective-permute-start | bytes 393224 | tf_op jit(solution)/shard_map/ppermute | solution.py:161
  30.2 7.6 %collective-permute-start.11 = (bf16[256,256]{1,0:T(8,128)(2,1)S(1)}, bf16[256,256]{1,0:T(8,128)(2,1)S(1)}, u32[]{:S(2)}, u32[]{:S(2)}) collective-permute-start(bf16[256,256]{1,0:T(8,128)(2,1)S(1)} %get-tuple-element.8), channel_id=1, source_target_pairs={{0,14},{1,15},{2,0},{3,1},{4,2},{5,3},{6,4},{7,5},{8,6},{9,7},{10,... | collective-permute-start | bytes 393224 | tf_op jit(solution)/shard_map/ppermute | solution.py:161
  38.5 4.8 %collective-permute-start.12 = (bf16[8,256,256]{2,1,0:T(8,128)(2,1)}, bf16[8,256,256]{2,1,0:T(8,128)(2,1)S(1)}, u32[]{:S(2)}, u32[]{:S(2)}) collective-permute-start(bf16[8,256,256]{2,1,0:T(8,128)(2,1)} %get-tuple-element.12), channel_id=1, source_target_pairs={{0,1},{1,0},{2,3},{3,2},{4,5},{5,4},{6,7},{7,6},{8,9},{9,8},{10,11... | collective-permute-start | bytes 3145736 | tf_op jit(solution)/shard_map/ppermute | solution.py:152
  54.1 1.3 %copy-start.1 = (bf16[16,256,256]{2,1,0:T(8,128)(2,1)}, bf16[16,256,256]{2,1,0:T(8,128)(2,1)S(1)}, u32[]{:S(2)}) copy-start(bf16[16,256,256]{2,1,0:T(8,128)(2,1)S(1)} %all-to-all-done.features_ref) | copy-start | bytes 6291460
  59.8 37.3 %all-to-all-start.1 = ((bf16[16,272,256]{2,1,0:T(8,128)(2,1)}), bf16[16,272,256]{2,1,0:T(8,128)(2,1)S(1)}, u32[]{:S(2)}, u32[]{:S(2)}) async-start(bf16[16,272,256]{2,1,0:T(8,128)(2,1)} %pack.1), calls=%async_computation.1 | async-start | bytes 4456448 | tf_op jit(solution)/shard_map/all_to_all | solution.py:198
  76.7 2.9 %collective-permute-start = (bf16[16,128,256]{2,1,0:T(8,128)(2,1)}, bf16[16,128,256]{2,1,0:T(8,128)(2,1)S(1)}, u32[]{:S(2)}, u32[]{:S(2)}) collective-permute-start(bf16[16,128,256]{2,1,0:T(8,128)(2,1)} %get-tuple-element.6), channel_id=1, source_target_pairs={{0,1},{1,0},{2,3},{3,2},{4,5},{5,4},{6,7},{7,6},{8,9},{9,8},{10,11... | collective-permute-start | bytes 3145736 | tf_op jit(solution)/shard_map/ppermute | solution.py:152
  81.9 23.0 %collective-permute-start.1 = (bf16[4,256,256]{2,1,0:T(8,128)(2,1)}, bf16[4,256,256]{2,1,0:T(8,128)(2,1)}, u32[]{:S(2)}, u32[]{:S(2)}) collective-permute-start(bf16[4,256,256]{2,1,0:T(8,128)(2,1)} %bitcast.7), channel_id=1, source_target_pairs={{0,2},{1,3},{2,0},{3,1},{4,6},{5,7},{6,4},{7,5},{8,10},{9,11},{10,... | collective-permute-start | bytes 1572872 | tf_op jit(solution)/shard_map/ppermute | solution.py:156
  97.5 0.7 copy-start.2
  98.9 18.0 %all-to-all-start.2 = ((f32[16,16,256]{2,1,0:T(8,128)}), f32[16,16,256]{2,1,0:T(8,128)S(1)}, u32[]{:S(2)}, u32[]{:S(2)}) async-start(f32[16,16,256]{2,1,0:T(8,128)} %broadcast_in_dim.13), calls=%async_computation.2 | async-start | bytes 524288 | tf_op jit(solution)/shard_map/all_to_all | solution.py:148
  106.1 20.5 %copy-start.3 = (f32[272,256]{1,0:T(8,128)S(1)}, f32[272,256]{1,0:T(8,128)}, u32[]{:S(2)}) copy-start(f32[272,256]{1,0:T(8,128)} %copy-done.2) | copy-start | bytes 835588
  106.1 18.2 %collective-permute-start.2 = (bf16[256,256]{1,0:T(8,128)(2,1)S(1)}, bf16[256,256]{1,0:T(8,128)(2,1)S(1)}, u32[]{:S(2)}, u32[]{:S(2)}) collective-permute-start(bf16[256,256]{1,0:T(8,128)(2,1)S(1)} %get-tuple-element.9), channel_id=1, source_target_pairs={{0,4},{1,5},{2,6},{3,7},{4,8},{5,9},{6,10},{7,11},{8,12},{9,13},{1... | collective-permute-start | bytes 393224 | tf_op jit(solution)/shard_map/ppermute | solution.py:161
  108.5 17.2 %collective-permute-start.3 = (bf16[256,256]{1,0:T(8,128)(2,1)S(1)}, bf16[256,256]{1,0:T(8,128)(2,1)S(1)}, u32[]{:S(2)}, u32[]{:S(2)}) collective-permute-start(bf16[256,256]{1,0:T(8,128)(2,1)S(1)} %get-tuple-element.11), channel_id=1, source_target_pairs={{0,8},{1,9},{2,10},{3,11},{4,12},{5,13},{6,14},{7,15},{8,0},{9,1},... | collective-permute-start | bytes 393224 | tf_op jit(solution)/shard_map/ppermute | solution.py:161
  111.8 13.9 %collective-permute-start.4 = (bf16[256,256]{1,0:T(8,128)(2,1)S(1)}, bf16[256,256]{1,0:T(8,128)(2,1)S(1)}, u32[]{:S(2)}, u32[]{:S(2)}) collective-permute-start(bf16[256,256]{1,0:T(8,128)(2,1)S(1)} %get-tuple-element.10), channel_id=1, source_target_pairs={{0,12},{1,13},{2,14},{3,15},{4,0},{5,1},{6,2},{7,3},{8,4},{9,5},{1... | collective-permute-start | bytes 393224 | tf_op jit(solution)/shard_map/ppermute | solution.py:161
  117.7 15.1 %all-to-all-start.3 = ((f32[16,16,256]{2,1,0:T(8,128)}), f32[16,16,256]{2,1,0:T(8,128)S(1)}, u32[]{:S(2)}, u32[]{:S(2)}) async-start(f32[16,16,256]{2,1,0:T(8,128)} %broadcast_in_dim.14), calls=%async_computation.3 | async-start | bytes 524288 | tf_op jit(solution)/shard_map/all_to_all | solution.py:148

commit v2 on v1

--- a/solution.py
+++ b/solution.py
@@ -8,7 +8,7 @@
 from jax.sharding import PartitionSpec as P
 
 BLOCK = 64
-VMEM = 56 << 20
+VMEM = 24 << 20
 
 
 def unpack(words):
@@ -195,9 +195,10 @@
         count, col_targets, row_sources, bits, gradient.reshape(-1, tile, width)
     )
     partial = pack(partial.reshape(n_row, nodes, width), source)
+
+    late, partial = lax.optimization_barrier((source, partial))
     shares = lax.all_to_all(partial, "row", 0, 0)
-
-    kept, sent = forward_sweep(count, row_targets, col_ids, bits, source.reshape(-1, tile, width))
+    kept, sent = forward_sweep(count, row_targets, col_ids, bits, late.reshape(-1, tile, width))
     chip = kept.astype(jnp.float32) + swap_cores(sent).astype(jnp.float32)
     chip = chip.reshape(2, n_z // 2, nodes, width)
     got = swap_chips(chip[1].astype(jnp.bfloat16))

time: 134 us -> 133 us (level)
  Pallas kernels: 24.1 us -> 13.7 us
  waiting for transfers between devices: 28.5 us -> 31.9 us
  starting transfers between devices: 56.7 us -> 59.8 us
  local copies, waits for them, and re-layouts: 14.5 us -> 16.7 us
    pallas_call x1, Pallas kernels: 10 us -> 3.96 us  [forward_sweep(): pl.pallas_call(forward_body, out_shape=(out, out), grid_spec=pltpu.Prefet...]
    pallas_call x1, Pallas kernels: 9.72 us -> 5.4 us  [backward_sweep(): pl.pallas_call(backward_body, out_shape=out, grid_spec=pltpu.PrefetchScal...]
    all_to_all x2, waiting for transfers between devices: 7.19 us -> 4.36 us  [spread(): lax.all_to_all(jnp.broadcast_to(block[None], (copies, *block.shape)), axi...]
    ppermute x10, waiting for transfers between devices: 4.61 us -> 7.37 us  [from_below(): lax.ppermute(block, 'col', [(i, (i + 2 * distance) % n_col) for i in rang...]
    unnamed x20 -> x24, local copies, waits for them, and re-layouts: 7.81 us -> 10.1 us
    all_to_all x1, waiting for transfers between devices: 13.5 us -> 15.4 us  [per_device(): shares = lax.all_to_all(partial, 'row', 0, 0)]
    reduce_sum x1, other arithmetic: 0.33 us -> 1.97 us  [per_device(): shares = shares.astype(jnp.float32).sum(0)]
    all_to_all x1, starting transfers between devices: 6.79 us -> 8.38 us  [per_device(): shares = lax.all_to_all(partial, 'row', 0, 0)]
  transfers between devices with their start and end apart: 17 -> 17, of which waited for: 8 -> 9; matrix products, arithmetic and copies ran while one was open for 13% -> 13% of each run, Pallas kernels for 15% -> 7%
where the time goes in v2:
time: 133 us; the launch traced here: 131 us
  starting transfers between devices  59.8 us (45%)
  waiting for transfers between devices  31.9 us (24%)
  local copies, waits for them, and re-layouts  16.7 us (13%)
  Pallas kernels  13.7 us (10%)
  other arithmetic  5.88 us (4%)
  matrix products  1.77 us (1%)
  between operations  1.48 us (1%)
    ppermute x10, starting transfers between devices, from_below(): lax.ppermute(block, 'col', [(i, (i + 2 * distance) % n_col) for i in rang...  26.2 us
    all_to_all x1, waiting for transfers between devices, per_device(): shares = lax.all_to_all(partial, 'row', 0, 0)  15.4 us
    all_to_all x2, starting transfers between devices, spread(): lax.all_to_all(jnp.broadcast_to(block[None], (copies, *block.shape)), axi...  13.6 us
    unnamed x24, local copies, waits for them, and re-layouts  10.1 us
    all_to_all x1, starting transfers between devices, per_device(): shares = lax.all_to_all(partial, 'row', 0, 0)  8.38 us
    ppermute x10, waiting for transfers between devices, from_below(): lax.ppermute(block, 'col', [(i, (i + 2 * distance) % n_col) for i in rang...  7.37 us
    all_to_all x1, starting transfers between devices, per_device(): source = lax.all_to_all(copies, 'row', 0, 0)  6.75 us
    pallas_call x1, Pallas kernels, backward_sweep(): pl.pallas_call(backward_body, out_shape=out, grid_spec=pltpu.PrefetchScal...  5.4 us
  transfers between devices with their start and end apart: 17, of which 9 were waited for; matrix products, arithmetic and copies ran while one was open for 13% of the time, Pallas kernels for 7%

profile of v2, /device:TPU:1, one launch (start us, length us, event | category | flops | bytes accessed | tf_op | source)
XLA Modules:
  0.0 131.3 jit_solution(5014850970161639044)
XLA Ops:
  1.4 1.7 %bitcast_dynamic-update-slice_fusion.15 = (bf16[8,256,256]{2,1,0:T(8,128)(2,1)}, bf16[256,256]{1,0:T(8,128)(2,1)S(1)}) fusion(f32[256]{0:T(256)S(1)} %convert_element_type.56, bf16[256,256]{1,0:T(8,128)(2,1)} %param.9), kind=kLoop, calls=%fused_computation.33 | loop fusion | flops 196607 | bytes 394240
  3.0 2.5 %collective-permute-start = (bf16[256,256]{1,0:T(8,128)(2,1)S(1)}, bf16[256,256]{1,0:T(8,128)(2,1)S(1)}, u32[]{:S(2)}, u32[]{:S(2)}) collective-permute-start(bf16[256,256]{1,0:T(8,128)(2,1)S(1)} %get-tuple-element.12), channel_id=1, source_target_pairs={{0,2},{1,3},{2,4},{3,5},{4,6},{5,7},{6,8},{7,9},{8,10},{9,11},{10,... | collective-permute-start | bytes 393224 | tf_op jit(solution)/shard_map/ppermute | solution.py:161
  5.5 3.0 %collective-permute-start.1 = (bf16[256,256]{1,0:T(8,128)(2,1)S(1)}, bf16[256,256]{1,0:T(8,128)(2,1)S(1)}, u32[]{:S(2)}, u32[]{:S(2)}) collective-permute-start(bf16[256,256]{1,0:T(8,128)(2,1)S(1)} %get-tuple-element.12), channel_id=1, source_target_pairs={{0,4},{1,5},{2,6},{3,7},{4,8},{5,9},{6,10},{7,11},{8,12},{9,13},{1... | collective-permute-start | bytes 393224 | tf_op jit(solution)/shard_map/ppermute | solution.py:161
  8.5 3.8 %collective-permute-start.2 = (bf16[256,256]{1,0:T(8,128)(2,1)S(1)}, bf16[256,256]{1,0:T(8,128)(2,1)S(1)}, u32[]{:S(2)}, u32[]{:S(2)}) collective-permute-start(bf16[256,256]{1,0:T(8,128)(2,1)S(1)} %get-tuple-element.12), channel_id=1, source_target_pairs={{0,6},{1,7},{2,8},{3,9},{4,10},{5,11},{6,12},{7,13},{8,14},{9,15},... | collective-permute-start | bytes 393224 | tf_op jit(solution)/shard_map/ppermute | solution.py:161
  12.7 4.5 %collective-permute-start.4 = (bf16[256,256]{1,0:T(8,128)(2,1)S(1)}, bf16[256,256]{1,0:T(8,128)(2,1)S(1)}, u32[]{:S(2)}, u32[]{:S(2)}) collective-permute-start(bf16[256,256]{1,0:T(8,128)(2,1)S(1)} %get-tuple-element.12), channel_id=1, source_target_pairs={{0,10},{1,11},{2,12},{3,13},{4,14},{5,15},{6,0},{7,1},{8,2},{9,3},... | collective-permute-start | bytes 393224 | tf_op jit(solution)/shard_map/ppermute | solution.py:161
  17.2 2.5 %broadcast_in_dim.12 = bf16[16,256,256]{2,1,0:T(8,128)(2,1)} broadcast(bf16[256,256]{1,0:T(8,128)(2,1)} %param.8), dimensions={1,2} | broadcast | bytes 2228224 | tf_op jit(solution)/shard_map/broadcast_in_dim | solution.py:178
  19.6 6.8 %all-to-all-start = ((bf16[16,256,256]{2,1,0:T(8,128)(2,1)}), bf16[16,256,256]{2,1,0:T(8,128)(2,1)S(1)}, u32[]{:S(2)}, u32[]{:S(2)}) async-start(bf16[16,256,256]{2,1,0:T(8,128)(2,1)} %broadcast_in_dim.12), calls=%async_computation | async-start | bytes 4194304 | tf_op jit(solution)/shard_map/all_to_all | solution.py:179
  27.1 2.4 %collective-permute-start.5 = (bf16[256,256]{1,0:T(8,128)(2,1)S(1)}, bf16[256,256]{1,0:T(8,128)(2,1)S(1)}, u32[]{:S(2)}, u32[]{:S(2)}) collective-permute-start(bf16[256,256]{1,0:T(8,128)(2,1)S(1)} %get-tuple-element.12), channel_id=1, source_target_pairs={{0,12},{1,13},{2,14},{3,15},{4,0},{5,1},{6,2},{7,3},{8,4},{9,5},{1... | collective-permute-start | bytes 393224 | tf_op jit(solution)/shard_map/ppermute | solution.py:161
  33.9 2.1 %collective-permute-done.5 = bf16[256,256]{1,0:T(8,128)(2,1)S(1)} collective-permute-done((bf16[256,256]{1,0:T(8,128)(2,1)S(1)}, bf16[256,256]{1,0:T(8,128)(2,1)S(1)}, u32[]{:S(2)}, u32[]{:S(2)}) %collective-permute-start.5) | collective-permute-done | bytes 131104 | tf_op jit(solution)/shard_map/ppermute | solution.py:161
  38.5 2.3 %collective-permute-start.7 = (bf16[8,256,256]{2,1,0:T(8,128)(2,1)}, bf16[8,256,256]{2,1,0:T(8,128)(2,1)S(1)}, u32[]{:S(2)}, u32[]{:S(2)}) collective-permute-start(bf16[8,256,256]{2,1,0:T(8,128)(2,1)} %get-tuple-element.16), channel_id=1, source_target_pairs={{0,1},{1,0},{2,3},{3,2},{4,5},{5,4},{6,7},{7,6},{8,9},{9,8},{10,11... | collective-permute-start | bytes 3145736 | tf_op jit(solution)/shard_map/ppermute | solution.py:152
  41.6 1.8 %collective-permute-done.7 = bf16[8,256,256]{2,1,0:T(8,128)(2,1)S(1)} collective-permute-done((bf16[8,256,256]{2,1,0:T(8,128)(2,1)}, bf16[8,256,256]{2,1,0:T(8,128)(2,1)S(1)}, u32[]{:S(2)}, u32[]{:S(2)}) %collective-permute-start.7) | collective-permute-done | bytes 1048608 | tf_op jit(solution)/shard_map/ppermute | solution.py:152
  43.3 1.1 constant_dynamic-update-slice_fusion
  44.4 5.4 %backward_sweep.1 = bf16[32,128,256]{2,1,0:T(8,128)(2,1)S(1)} custom-call(s32[1]{0:T(128)} %bitcast.53.count_ref, s32[256]{0:T(256)S(1)} %get-tuple-element.32.to_ref, s32[256]{0:T(256)S(1)} %get-tuple-element.30.from_ref, s32[256,16,128]{2,1,0:T(8,128)S(1)} %bitcast.60, bf16[32,128,256]{2,1,0:T(8,128)(2,1)} %bitcast.13.source_ref), custom_call_target="tpu_custom_call" | custom-call | flops 2147483648 | bytes 6291456 | tf_op jit(solution)/shard_map/backward_sweep/pallas_call | solution.py:92
  49.8 1.3 %copy-done.3 = bf16[32,128,256]{2,1,0:T(8,128)(2,1)} copy-done((bf16[32,128,256]{2,1,0:T(8,128)(2,1)}, bf16[32,128,256]{2,1,0:T(8,128)(2,1)S(1)}, u32[]{:S(2)}) %copy-start.3) | copy-done | bytes 2097176
  51.8 1.4 %copy-done.1 = bf16[16,256,256]{2,1,0:T(8,128)(2,1)} copy-done((bf16[16,256,256]{2,1,0:T(8,128)(2,1)}, bf16[16,256,256]{2,1,0:T(8,128)(2,1)S(1)}, u32[]{:S(2)}) %copy-start.1) | copy-done | bytes 2097176
  53.2 4.4 %pack.1 = bf16[16,272,256]{2,1,0:T(8,128)(2,1)} custom-call(bf16[16,256,256]{2,1,0:T(8,128)(2,1)} %bitcast.57, bf16[16,256,256]{2,1,0:T(8,128)(2,1)} %copy-done.1), custom_call_target="tpu_custom_call" | custom-call | flops 536870912 | bytes 6291456 | tf_op jit(solution)/shard_map/pack/pallas_call | solution.py:134
  57.6 8.4 %all-to-all-start.1 = ((bf16[16,272,256]{2,1,0:T(8,128)(2,1)}), bf16[16,272,256]{2,1,0:T(8,128)(2,1)}, u32[]{:S(2)}, u32[]{:S(2)}) async-start(bf16[16,272,256]{2,1,0:T(8,128)(2,1)} %pack.1), calls=%async_computation.1 | async-start | bytes 4456448 | tf_op jit(solution)/shard_map/all_to_all | solution.py:200
  66.0 1.6 %copy-done.6 = s32[1,1,256,16,128]{4,3,2,1,0:T(8,128)S(1)} copy-done((s32[1,1,256,16,128]{4,3,2,1,0:T(8,128)S(1)}, s32[1,1,256,16,128]{4,3,2,1,0:T(8,128)}, u32[]{:S(2)}) %copy-start.6) | copy-done | bytes 2097176
  67.5 4.0 %forward_sweep.1 = (bf16[16,128,256]{2,1,0:T(8,128)(2,1)S(1)}, bf16[16,128,256]{2,1,0:T(8,128)(2,1)S(1)}) custom-call(s32[1]{0:T(128)} %bitcast.54.count_ref, s32[256]{0:T(256)S(1)} %get-tuple-element.31.to_ref, s32[256]{0:T(256)S(1)} %bitcast.59, s32[256,16,128]{2,1,0:T(8,128)S(1)} %bitcast.61, bf16[32,128,256]{2,1,0:T(8,128)(2,1)S(1)} %bitcast.56), custom_call_target="tpu_custom_call" | custom-call | flops 2147483648 | bytes 6291456 | tf_op jit(solution)/shard_map/forward_sweep/pallas_call | solution.py:57
  71.5 1.7 %collective-permute-start.8 = (bf16[16,128,256]{2,1,0:T(8,128)(2,1)S(1)}, bf16[16,128,256]{2,1,0:T(8,128)(2,1)S(1)}, u32[]{:S(2)}, u32[]{:S(2)}) collective-permute-start(bf16[16,128,256]{2,1,0:T(8,128)(2,1)S(1)} %get-tuple-element.9), channel_id=1, source_target_pairs={{0,1},{1,0},{2,3},{3,2},{4,5},{5,4},{6,7},{7,6},{8,9},{9,8},{10,11... | collective-permute-start | bytes 3145736 | tf_op jit(solution)/shard_map/ppermute | solution.py:152
  73.3 2.3 %collective-permute-done.8 = bf16[16,128,256]{2,1,0:T(8,128)(2,1)S(1)} collective-permute-done((bf16[16,128,256]{2,1,0:T(8,128)(2,1)S(1)}, bf16[16,128,256]{2,1,0:T(8,128)(2,1)S(1)}, u32[]{:S(2)}, u32[]{:S(2)}) %collective-permute-start.8) | collective-permute-done | bytes 1048608 | tf_op jit(solution)/shard_map/ppermute | solution.py:152
  77.6 15.4 %all-to-all-done.1 = bf16[16,272,256]{2,1,0:T(8,128)(2,1)} async-done(((bf16[16,272,256]{2,1,0:T(8,128)(2,1)}), bf16[16,272,256]{2,1,0:T(8,128)(2,1)}, u32[]{:S(2)}, u32[]{:S(2)}) %all-to-all-start.1) | async-done | bytes 2228256 | tf_op jit(solution)/shard_map/all_to_all | solution.py:200
  93.1 2.0 %convert_reduce_fusion = f32[272,256]{1,0:T(8,128)S(1)} fusion(bf16[16,272,256]{2,1,0:T(8,128)(2,1)} %all-to-all-done.1), kind=kLoop, calls=%fused_computation | loop fusion | flops 2158592 | bytes 2506752 | tf_op jit(solution)/shard_map/reduce_sum | solution.py:209
  95.8 9.7 %all-to-all-start.2 = ((f32[16,16,256]{2,1,0:T(8,128)}), f32[16,16,256]{2,1,0:T(8,128)S(1)}, u32[]{:S(2)}, u32[]{:S(2)}) async-start(f32[16,16,256]{2,1,0:T(8,128)} %broadcast_in_dim.13), calls=%async_computation.2 | async-start | bytes 524288 | tf_op jit(solution)/shard_map/all_to_all | solution.py:148
  105.5 1.2 fusion
  106.8 2.4 %collective-permute-start.10 = (bf16[256,256]{1,0:T(8,128)(2,1)S(1)}, bf16[256,256]{1,0:T(8,128)(2,1)S(1)}, u32[]{:S(2)}, u32[]{:S(2)}) collective-permute-start(bf16[256,256]{1,0:T(8,128)(2,1)S(1)} %get-tuple-element.13), channel_id=1, source_target_pairs={{0,4},{1,5},{2,6},{3,7},{4,8},{5,9},{6,10},{7,11},{8,12},{9,13},{1... | collective-permute-start | bytes 393224 | tf_op jit(solution)/shard_map/ppermute | solution.py:161
  109.2 3.3 %collective-permute-start.11 = (bf16[256,256]{1,0:T(8,128)(2,1)S(1)}, bf16[256,256]{1,0:T(8,128)(2,1)S(1)}, u32[]{:S(2)}, u32[]{:S(2)}) collective-permute-start(bf16[256,256]{1,0:T(8,128)(2,1)S(1)} %get-tuple-element.15), channel_id=1, source_target_pairs={{0,8},{1,9},{2,10},{3,11},{4,12},{5,13},{6,14},{7,15},{8,0},{9,1},... | collective-permute-start | bytes 393224 | tf_op jit(solution)/shard_map/ppermute | solution.py:161
  112.5 3.3 %collective-permute-start.12 = (bf16[256,256]{1,0:T(8,128)(2,1)S(1)}, bf16[256,256]{1,0:T(8,128)(2,1)S(1)}, u32[]{:S(2)}, u32[]{:S(2)}) collective-permute-start(bf16[256,256]{1,0:T(8,128)(2,1)S(1)} %get-tuple-element.14), channel_id=1, source_target_pairs={{0,12},{1,13},{2,14},{3,15},{4,0},{5,1},{6,2},{7,3},{8,4},{9,5},{1... | collective-permute-start | bytes 393224 | tf_op jit(solution)/shard_map/ppermute | solution.py:161
  115.7 1.8 %all-to-all-done.2 = f32[16,16,256]{2,1,0:T(8,128)S(1)} async-done(((f32[16,16,256]{2,1,0:T(8,128)}), f32[16,16,256]{2,1,0:T(8,128)S(1)}, u32[]{:S(2)}, u32[]{:S(2)}) %all-to-all-start.2) | async-done | bytes 262176 | tf_op jit(solution)/shard_map/all_to_all | solution.py:148
  118.3 3.8 %all-to-all-start.3 = ((f32[16,16,256]{2,1,0:T(8,128)}), f32[16,16,256]{2,1,0:T(8,128)S(1)}, u32[]{:S(2)}, u32[]{:S(2)}) async-start(f32[16,16,256]{2,1,0:T(8,128)} %broadcast_in_dim.14), calls=%async_computation.3 | async-start | bytes 524288 | tf_op jit(solution)/shard_map/all_to_all | solution.py:148
  122.2 4.2 %collective-permute-done.11 = bf16[256,256]{1,0:T(8,128)(2,1)S(1)} collective-permute-done((bf16[256,256]{1,0:T(8,128)(2,1)S(1)}, bf16[256,256]{1,0:T(8,128)(2,1)S(1)}, u32[]{:S(2)}, u32[]{:S(2)}) %collective-permute-start.11) | collective-permute-done | bytes 131104 | tf_op jit(solution)/shard_map/ppermute | solution.py:161
  128.1 2.5 %all-to-all-done.3 = f32[16,16,256]{2,1,0:T(8,128)S(1)} async-done(((f32[16,16,256]{2,1,0:T(8,128)}), f32[16,16,256]{2,1,0:T(8,128)S(1)}, u32[]{:S(2)}, u32[]{:S(2)}) %all-to-all-start.3) | async-done | bytes 262176 | tf_op jit(solution)/shard_map/all_to_all | solution.py:148
  (47 shorter events, 15.6 us)
Async XLA Ops:
  0.6 125.7 %copy-start = (bf16[256,256]{1,0:T(8,128)(2,1)S(1)}, bf16[256,256]{1,0:T(8,128)(2,1)}, u32[]{:S(2)}) copy-start(bf16[256,256]{1,0:T(8,128)(2,1)} %param.11) | copy-start | bytes 393220
  3.0 24.1 %collective-permute-start = (bf16[256,256]{1,0:T(8,128)(2,1)S(1)}, bf16[256,256]{1,0:T(8,128)(2,1)S(1)}, u32[]{:S(2)}, u32[]{:S(2)}) collective-permute-start(bf16[256,256]{1,0:T(8,128)(2,1)S(1)} %get-tuple-element.12), channel_id=1, source_target_pairs={{0,2},{1,3},{2,4},{3,5},{4,6},{5,7},{6,8},{7,9},{8,10},{9,11},{10,... | collective-permute-start | bytes 393224 | tf_op jit(solution)/shard_map/ppermute | solution.py:161
  5.5 24.7 %collective-permute-start.1 = (bf16[256,256]{1,0:T(8,128)(2,1)S(1)}, bf16[256,256]{1,0:T(8,128)(2,1)S(1)}, u32[]{:S(2)}, u32[]{:S(2)}) collective-permute-start(bf16[256,256]{1,0:T(8,128)(2,1)S(1)} %get-tuple-element.12), channel_id=1, source_target_pairs={{0,4},{1,5},{2,6},{3,7},{4,8},{5,9},{6,10},{7,11},{8,12},{9,13},{1... | collective-permute-start | bytes 393224 | tf_op jit(solution)/shard_map/ppermute | solution.py:161
  8.5 23.2 %collective-permute-start.2 = (bf16[256,256]{1,0:T(8,128)(2,1)S(1)}, bf16[256,256]{1,0:T(8,128)(2,1)S(1)}, u32[]{:S(2)}, u32[]{:S(2)}) collective-permute-start(bf16[256,256]{1,0:T(8,128)(2,1)S(1)} %get-tuple-element.12), channel_id=1, source_target_pairs={{0,6},{1,7},{2,8},{3,9},{4,10},{5,11},{6,12},{7,13},{8,14},{9,15},... | collective-permute-start | bytes 393224 | tf_op jit(solution)/shard_map/ppermute | solution.py:161
  12.2 20.2 %collective-permute-start.3 = (bf16[256,256]{1,0:T(8,128)(2,1)S(1)}, bf16[256,256]{1,0:T(8,128)(2,1)S(1)}, u32[]{:S(2)}, u32[]{:S(2)}) collective-permute-start(bf16[256,256]{1,0:T(8,128)(2,1)S(1)} %get-tuple-element.12), channel_id=1, source_target_pairs={{0,8},{1,9},{2,10},{3,11},{4,12},{5,13},{6,14},{7,15},{8,0},{9,1},... | collective-permute-start | bytes 393224 | tf_op jit(solution)/shard_map/ppermute | solution.py:161
  12.7 20.5 %collective-permute-start.4 = (bf16[256,256]{1,0:T(8,128)(2,1)S(1)}, bf16[256,256]{1,0:T(8,128)(2,1)S(1)}, u32[]{:S(2)}, u32[]{:S(2)}) collective-permute-start(bf16[256,256]{1,0:T(8,128)(2,1)S(1)} %get-tuple-element.12), channel_id=1, source_target_pairs={{0,10},{1,11},{2,12},{3,13},{4,14},{5,15},{6,0},{7,1},{8,2},{9,3},... | collective-permute-start | bytes 393224 | tf_op jit(solution)/shard_map/ppermute | solution.py:161
  19.6 32.2 %all-to-all-start = ((bf16[16,256,256]{2,1,0:T(8,128)(2,1)}), bf16[16,256,256]{2,1,0:T(8,128)(2,1)S(1)}, u32[]{:S(2)}, u32[]{:S(2)}) async-start(bf16[16,256,256]{2,1,0:T(8,128)(2,1)} %broadcast_in_dim.12), calls=%async_computation | async-start | bytes 4194304 | tf_op jit(solution)/shard_map/all_to_all | solution.py:179
  26.4 15.1 %copy-start.4 = (s32[1,1,256]{2,1,0:T(1,128)S(1)}, s32[1,1,256]{2,1,0:T(1,128)}, u32[]{:S(2)}) copy-start(s32[1,1,256]{2,1,0:T(1,128)} %param.13) | copy-start | bytes 3076
  26.4 15.1 %copy-start.7 = (s32[1,1,256]{2,1,0:T(1,128)S(1)}, s32[1,1,256]{2,1,0:T(1,128)}, u32[]{:S(2)}) copy-start(s32[1,1,256]{2,1,0:T(1,128)} %param.12) | copy-start | bytes 3076
  27.1 8.9 %collective-permute-start.5 = (bf16[256,256]{1,0:T(8,128)(2,1)S(1)}, bf16[256,256]{1,0:T(8,128)(2,1)S(1)}, u32[]{:S(2)}, u32[]{:S(2)}) collective-permute-start(bf16[256,256]{1,0:T(8,128)(2,1)S(1)} %get-tuple-element.12), channel_id=1, source_target_pairs={{0,12},{1,13},{2,14},{3,15},{4,0},{5,1},{6,2},{7,3},{8,4},{9,5},{1... | collective-permute-start | bytes 393224 | tf_op jit(solution)/shard_map/ppermute | solution.py:161
  30.2 7.6 %collective-permute-start.6 = (bf16[256,256]{1,0:T(8,128)(2,1)S(1)}, bf16[256,256]{1,0:T(8,128)(2,1)S(1)}, u32[]{:S(2)}, u32[]{:S(2)}) collective-permute-start(bf16[256,256]{1,0:T(8,128)(2,1)S(1)} %get-tuple-element.12), channel_id=1, source_target_pairs={{0,14},{1,15},{2,0},{3,1},{4,2},{5,3},{6,4},{7,5},{8,6},{9,7},{10,... | collective-permute-start | bytes 393224 | tf_op jit(solution)/shard_map/ppermute | solution.py:161
  38.5 4.8 %collective-permute-start.7 = (bf16[8,256,256]{2,1,0:T(8,128)(2,1)}, bf16[8,256,256]{2,1,0:T(8,128)(2,1)S(1)}, u32[]{:S(2)}, u32[]{:S(2)}) collective-permute-start(bf16[8,256,256]{2,1,0:T(8,128)(2,1)} %get-tuple-element.16), channel_id=1, source_target_pairs={{0,1},{1,0},{2,3},{3,2},{4,5},{5,4},{6,7},{7,6},{8,9},{9,8},{10,11... | collective-permute-start | bytes 3145736 | tf_op jit(solution)/shard_map/ppermute | solution.py:152
  41.5 2.9 %copy-start.5 = (s32[1,1,256,16,128]{4,3,2,1,0:T(8,128)S(1)}, s32[1,1,256,16,128]{4,3,2,1,0:T(8,128)}, u32[]{:S(2)}) copy-start(s32[1,1,256,16,128]{4,3,2,1,0:T(8,128)} %param.14) | copy-start | bytes 6291460
  49.8 1.3 %copy-start.3 = (bf16[32,128,256]{2,1,0:T(8,128)(2,1)}, bf16[32,128,256]{2,1,0:T(8,128)(2,1)S(1)}, u32[]{:S(2)}) copy-start(bf16[32,128,256]{2,1,0:T(8,128)(2,1)S(1)} %backward_sweep.1) | copy-start | bytes 6291460
  51.8 1.4 %copy-start.1 = (bf16[16,256,256]{2,1,0:T(8,128)(2,1)}, bf16[16,256,256]{2,1,0:T(8,128)(2,1)S(1)}, u32[]{:S(2)}) copy-start(bf16[16,256,256]{2,1,0:T(8,128)(2,1)S(1)} %all-to-all-done.features_ref) | copy-start | bytes 6291460
  57.5 8.4 %copy-start.2 = (bf16[16,256,256]{2,1,0:T(8,128)(2,1)S(1)}, bf16[16,256,256]{2,1,0:T(8,128)(2,1)}, u32[]{:S(2)}) copy-start(bf16[16,256,256]{2,1,0:T(8,128)(2,1)} %copy-done.1) | copy-start | bytes 6291460
  57.6 35.5 %all-to-all-start.1 = ((bf16[16,272,256]{2,1,0:T(8,128)(2,1)}), bf16[16,272,256]{2,1,0:T(8,128)(2,1)}, u32[]{:S(2)}, u32[]{:S(2)}) async-start(bf16[16,272,256]{2,1,0:T(8,128)(2,1)} %pack.1), calls=%async_computation.1 | async-start | bytes 4456448 | tf_op jit(solution)/shard_map/all_to_all | solution.py:200
  65.9 1.6 %copy-start.6 = (s32[1,1,256,16,128]{4,3,2,1,0:T(8,128)S(1)}, s32[1,1,256,16,128]{4,3,2,1,0:T(8,128)}, u32[]{:S(2)}) copy-start(s32[1,1,256,16,128]{4,3,2,1,0:T(8,128)} %param.14) | copy-start | bytes 6291460
  71.5 4.0 %collective-permute-start.8 = (bf16[16,128,256]{2,1,0:T(8,128)(2,1)S(1)}, bf16[16,128,256]{2,1,0:T(8,128)(2,1)S(1)}, u32[]{:S(2)}, u32[]{:S(2)}) collective-permute-start(bf16[16,128,256]{2,1,0:T(8,128)(2,1)S(1)} %get-tuple-element.9), channel_id=1, source_target_pairs={{0,1},{1,0},{2,3},{3,2},{4,5},{5,4},{6,7},{7,6},{8,9},{9,8},{10,11... | collective-permute-start | bytes 3145736 | tf_op jit(solution)/shard_map/ppermute | solution.py:152
  76.7 28.9 %collective-permute-start.9 = (bf16[4,256,256]{2,1,0:T(8,128)(2,1)}, bf16[4,256,256]{2,1,0:T(8,128)(2,1)}, u32[]{:S(2)}, u32[]{:S(2)}) collective-permute-start(bf16[4,256,256]{2,1,0:T(8,128)(2,1)} %bitcast.17), channel_id=1, source_target_pairs={{0,2},{1,3},{2,0},{3,1},{4,6},{5,7},{6,4},{7,5},{8,10},{9,11},{10,... | collective-permute-start | bytes 1572872 | tf_op jit(solution)/shard_map/ppermute | solution.py:156
  95.8 21.8 %all-to-all-start.2 = ((f32[16,16,256]{2,1,0:T(8,128)}), f32[16,16,256]{2,1,0:T(8,128)S(1)}, u32[]{:S(2)}, u32[]{:S(2)}) async-start(f32[16,16,256]{2,1,0:T(8,128)} %broadcast_in_dim.13), calls=%async_computation.2 | async-start | bytes 524288 | tf_op jit(solution)/shard_map/all_to_all | solution.py:148
  106.8 15.4 %collective-permute-start.10 = (bf16[256,256]{1,0:T(8,128)(2,1)S(1)}, bf16[256,256]{1,0:T(8,128)(2,1)S(1)}, u32[]{:S(2)}, u32[]{:S(2)}) collective-permute-start(bf16[256,256]{1,0:T(8,128)(2,1)S(1)} %get-tuple-element.13), channel_id=1, source_target_pairs={{0,4},{1,5},{2,6},{3,7},{4,8},{5,9},{6,10},{7,11},{8,12},{9,13},{1... | collective-permute-start | bytes 393224 | tf_op jit(solution)/shard_map/ppermute | solution.py:161
  109.2 17.2 %collective-permute-start.11 = (bf16[256,256]{1,0:T(8,128)(2,1)S(1)}, bf16[256,256]{1,0:T(8,128)(2,1)S(1)}, u32[]{:S(2)}, u32[]{:S(2)}) collective-permute-start(bf16[256,256]{1,0:T(8,128)(2,1)S(1)} %get-tuple-element.15), channel_id=1, source_target_pairs={{0,8},{1,9},{2,10},{3,11},{4,12},{5,13},{6,14},{7,15},{8,0},{9,1},... | collective-permute-start | bytes 393224 | tf_op jit(solution)/shard_map/ppermute | solution.py:161
  112.5 13.9 %collective-permute-start.12 = (bf16[256,256]{1,0:T(8,128)(2,1)S(1)}, bf16[256,256]{1,0:T(8,128)(2,1)S(1)}, u32[]{:S(2)}, u32[]{:S(2)}) collective-permute-start(bf16[256,256]{1,0:T(8,128)(2,1)S(1)} %get-tuple-element.14), channel_id=1, source_target_pairs={{0,12},{1,13},{2,14},{3,15},{4,0},{5,1},{6,2},{7,3},{8,4},{9,5},{1... | collective-permute-start | bytes 393224 | tf_op jit(solution)/shard_map/ppermute | solution.py:161
  118.3 12.3 %all-to-all-start.3 = ((f32[16,16,256]{2,1,0:T(8,128)}), f32[16,16,256]{2,1,0:T(8,128)S(1)}, u32[]{:S(2)}, u32[]{:S(2)}) async-start(f32[16,16,256]{2,1,0:T(8,128)} %broadcast_in_dim.14), calls=%async_computation.3 | async-start | bytes 524288 | tf_op jit(solution)/shard_map/all_to_all | solution.py:148
